TPU v7x, 256 devices: a whole 4x4x8 slice. The times are simulated.
256 devices in a mesh: row: 16 (over z, core), col: 16 (over y, x).
Axes of the slice: x: 4, y: 4, z: 8, core: 2. Of those that a mesh axis runs over, the one named last changes fastest.
Arguments:
- start_block: float32 [4096, 64, 128], P(('row', 'col')), may hold values from -2700 to 2700
- tile_values: bfloat16 [65536, 128, 128], P(('row', 'col')), may hold values from -3.535534 to 3.535534
- tile_rows: int32 [65536], P(('row', 'col')), may hold values from 0 to 15
- tile_cols: int32 [65536], P(('row', 'col')), may hold values from 0 to 79
- tile_count: int32 [256], P(('row', 'col')), may hold values from 32 to 256, as said below
- send_rows: int32 [256, 256, 32], P(('row', 'col')), may hold values from 0 to 2047
- send_count: int32 [256, 256], P(('row', 'col')), may hold values from 16 to 32, as said below
- rotation: float32 [192, 64], replicated, may hold values from -0.4375 to 0.4375
Outputs:
- embedding: float32 [4096, 64, 128], P(('row', 'col'))
Inputs may be any that keep to these rules, and one draw needn't show every extreme that they name: `tile_cols`: source tiles below 16 are the partition's own row tiles, the others its halo tiles. `tile_count`: slots at or past the count are ignored; some partition fills all 256 slots. `send_count`: slots at or past the count carry zeros; every partition fills all 32 slots for some peer, and some partition receives 32 rows from every partition.
All inputs are finite; a program needn't handle non-finite values.
Results may differ from a plain program's by a relative error of at most 0.0029.
Values may be sent and summed in bfloat16 or wider, within the bound.
A program may use at most 64 MiB of HBM per device.

v0:
```python
import jax
import jax.numpy as jnp
from jax import lax
from jax.sharding import PartitionSpec as P

HIGHEST_PRECISION = lax.Precision.HIGHEST


def local_inner(left_block, right_block):
    return jnp.einsum("tai,tbi->ab", left_block, right_block, precision=HIGHEST_PRECISION)


def unit_columns(product_block, gram_matrix):
    factor = jnp.linalg.cholesky(gram_matrix)
    inverse = lax.linalg.triangular_solve(
        factor, jnp.eye(factor.shape[0], dtype=jnp.float32), left_side=True, lower=True
    )
    return jnp.einsum("ab,tbi->tai", inverse, product_block, precision=HIGHEST_PRECISION)


def apply_graph(current, tile_values, tile_rows, tile_cols, tile_count, send_rows, send_count):
    row_tiles, block_width, tile_size = current.shape
    rounded = current.astype(jnp.bfloat16)
    node_rows = rounded.transpose(0, 2, 1).reshape(row_tiles * tile_size, block_width)
    targets = send_rows[0]
    partitions, capacity = targets.shape
    chosen = node_rows[targets.reshape(-1)].reshape(partitions, capacity, block_width)
    kept_slots = jnp.arange(capacity, dtype=jnp.int32)[None, :] < send_count[0][:, None]
    chosen = jnp.where(kept_slots[:, :, None], chosen, jnp.zeros_like(chosen))
    outgoing = chosen.reshape(lax.axis_size("row"), lax.axis_size("col"), capacity * block_width)
    incoming = lax.all_to_all(
        lax.all_to_all(outgoing, "row", split_axis=0, concat_axis=0, tiled=True),
        "col",
        split_axis=1,
        concat_axis=1,
        tiled=True,
    )
    halo_count = partitions * capacity // tile_size
    halo_block = incoming.reshape(halo_count, tile_size, block_width).transpose(0, 2, 1)
    source = jnp.concatenate([rounded, halo_block], 0)
    picked = source[tile_cols]
    products = jnp.einsum("kbj,kij->kbi", picked, tile_values, preferred_element_type=jnp.float32)
    slot_total = tile_cols.shape[0]
    live_slots = jnp.arange(slot_total, dtype=jnp.int32) < tile_count[0]
    owner_table = (
        tile_rows[None, :] == jnp.arange(row_tiles, dtype=jnp.int32)[:, None]
    ) & live_slots[None, :]
    return jnp.einsum(
        "rk,kbi->rbi", owner_table.astype(jnp.float32), products, precision=HIGHEST_PRECISION
    )


def body(
    start_block, tile_values, tile_rows, tile_cols, tile_count, send_rows, send_count, rotation
):
    node_total = (
        start_block.shape[0] * start_block.shape[2] * lax.axis_size("row") * lax.axis_size("col")
    )
    start_sum = lax.psum(local_inner(start_block, start_block), ("row", "col"))
    vectors = [unit_columns(start_block, start_sum / node_total)]
    for krylov_step in range(2):
        product_block = apply_graph(
            vectors[-1], tile_values, tile_rows, tile_cols, tile_count, send_rows, send_count
        )
        stacked = jnp.concatenate(vectors, 1)
        coefficients = lax.psum(local_inner(stacked, product_block), ("row", "col")) / node_total
        residual_block = product_block - jnp.einsum(
            "ab,tai->tbi", coefficients, stacked, precision=HIGHEST_PRECISION
        )
        gram_matrix = (
            lax.psum(local_inner(residual_block, residual_block), ("row", "col")) / node_total
        )
        vectors.append(unit_columns(residual_block, gram_matrix))
    all_vectors = jnp.concatenate(vectors, 1)
    return jnp.einsum("jb,tji->tbi", rotation, all_vectors, precision=HIGHEST_PRECISION)


def solution(mesh):
    return jax.shard_map(
        body,
        mesh=mesh,
        in_specs=(
            P(("row", "col"), None, None),
            P(("row", "col"), None, None),
            P(("row", "col")),
            P(("row", "col")),
            P(("row", "col")),
            P(("row", "col"), None, None),
            P(("row", "col"), None),
            P(),
        ),
        out_specs=P(("row", "col"), None, None),
        check_vma=False,
    )
```

profile of v0, /device:TPU:1, one launch (start us, length us, event | category | flops | bytes accessed | tf_op | source)
XLA Modules:
  0.0 668.5 jit_solution(7324829424072807957)
XLA Ops:
  0.0 1.0 copy-done
  1.6 81.5 %psum.35 = f32[64,64]{0,1:T(8,128)S(1)} all-reduce(f32[64,64]{0,1:T(8,128)S(1)} %convolution_bitcast_fusion.8), channel_id=1, replica_groups=mesh['row'=16,'col'=16] {'row','col'}, use_global_device_ids=true, to_apply=%region_0.0 | all-reduce | flops 4096 | bytes 32768 | tf_op jit(solution)/shard_map/psum | solution.py:59
  83.2 5.8 cholesky.59
  90.4 4.9 custom-call.7
  96.8 24.0 %gather_fusion = bf16[8192,64]{1,0:T(8,128)(2,1)S(1)} fusion(bf16[2048,64]{1,0:T(8,128)(2,1)S(1)} %bitcast.92, s32[8192]{0:T(1024)S(1)} %broadcast_clamp_fusion), kind=kCustom, calls=%fused_computation | custom fusion | bytes 2129920 | tf_op jit(solution)/shard_map/gather | solution.py:27
  120.9 2.4 reshape.93
  123.4 2.1 broadcast_in_dim.16
  125.5 1.8 broadcast_in_dim.17
  127.3 1.5 broadcast_select_fusion.1
  128.8 33.5 %all_to_all.20 = bf16[16,16,2048]{2,1,0:T(8,128)(2,1)S(1)} all-to-all(bf16[16,16,2048]{2,1,0:T(8,128)(2,1)S(1)} %broadcast_select_fusion.1), channel_id=1, replica_groups=mesh['row'=16,'col'=16] {'row'}, dimensions={0} | all-to-all | bytes 2097152 | tf_op jit(solution)/shard_map/all_to_all | solution.py:32
  162.3 1.6 copy.49
  163.9 3.9 all-to-all-start.1
  168.7 16.5 %all-to-all-done.1 = bf16[16,16,2048]{2,0,1:T(8,128)(2,1)S(1)} async-done(((bf16[16,16,2048]{2,0,1:T(8,128)(2,1)}), bf16[16,16,2048]{2,0,1:T(8,128)(2,1)S(1)}, u32[]{:S(2)}, u32[]{:S(2)}) %all-to-all-start.1) | async-done | bytes 1048608 | tf_op jit(solution)/shard_map/all_to_all | solution.py:31
  185.3 1.6 copy.50
  186.8 3.3 reshape.94
  190.2 2.1 pad_maximum_fusion
  192.2 10.4 %gather_fusion.1 = bf16[256,64,128]{1,2,0:T(8,128)(2,1)} fusion(bf16[80,64,128]{1,2,0:T(8,128)(2,1)} %pad_maximum_fusion, s32[1024]{0:T(1024)S(1)} %pad_clamp_fusion), kind=kCustom, calls=%fused_computation.1 | custom fusion | bytes 8389632 | tf_op jit(solution)/shard_map/gather | solution.py:41
  202.6 9.7 %fusion.57 = f32[256,64,128]{2,1,0:T(8,128)S(1)} fusion(bf16[256,64,128]{1,2,0:T(8,128)(2,1)} %gather_fusion.1, bf16[256,128,128]{2,1,0:T(8,128)(2,1)} %param.12), kind=kOutput, calls=%fused_computation.100 | convolution fusion | flops 536870912 | bytes 20971520 | tf_op jit(solution)/shard_map/kbj,kij->kbi/dot_general | solution.py:42
  212.3 7.5 %fusion.2 = f32[16,64,128]{2,0,1:T(8,128)S(1)} fusion(f32[256,64,128]{2,1,0:T(8,128)S(1)} %fusion.57, s32[256]{0:T(256)S(1)} %copy-done.6, pred[256]{0:T(512)(128)(4,1)S(1)} %iota_compare_fusion.7), kind=kOutput, calls=%fused_computation.6 | convolution fusion | flops 402661376 | bytes 8914176 | tf_op jit(solution)/shard_map/rk,kbi->rbi/dot_general | solution.py:48
  220.5 72.7 %psum.36 = f32[64,64]{0,1:T(8,128)S(1)} all-reduce(f32[64,64]{0,1:T(8,128)S(1)} %convolution_bitcast_fusion.6), channel_id=1, replica_groups=mesh['row'=16,'col'=16] {'row','col'}, use_global_device_ids=true, to_apply=%region_3.0 | all-reduce | flops 4096 | bytes 32768 | tf_op jit(solution)/shard_map/psum | solution.py:66
  294.2 0.7 convolution_bitcast_fusion.5
  295.0 73.9 %psum.37 = f32[64,64]{0,1:T(8,128)S(1)} all-reduce(f32[64,64]{0,1:T(8,128)S(1)} %convolution_bitcast_fusion.5), channel_id=1, replica_groups=mesh['row'=16,'col'=16] {'row','col'}, use_global_device_ids=true, to_apply=%region_4.0 | all-reduce | flops 4096 | bytes 32768 | tf_op jit(solution)/shard_map/psum | solution.py:71
  369.0 5.8 cholesky.70
  374.9 0.7 compare_reduce_fusion.1
  376.3 4.9 custom-call.8
  381.5 1.6 bitcast_convert_fusion
  383.3 24.0 %gather_fusion.2 = bf16[8192,64]{1,0:T(8,128)(2,1)S(1)} fusion(bf16[2048,64]{1,0:T(8,128)(2,1)S(1)} %bitcast.93, s32[8192]{0:T(1024)S(1)} %broadcast_clamp_fusion), kind=kCustom, calls=%fused_computation.2 | custom fusion | bytes 2129920 | tf_op jit(solution)/shard_map/gather | solution.py:27
  407.4 2.4 reshape.96
  409.8 1.5 broadcast_select_fusion
  411.3 32.6 %all_to_all.21 = bf16[16,16,2048]{2,1,0:T(8,128)(2,1)S(1)} all-to-all(bf16[16,16,2048]{2,1,0:T(8,128)(2,1)S(1)} %broadcast_select_fusion), channel_id=1, replica_groups=mesh['row'=16,'col'=16] {'row'}, dimensions={0} | all-to-all | bytes 2097152 | tf_op jit(solution)/shard_map/all_to_all | solution.py:32
  443.9 1.6 copy.64
  445.5 3.9 all-to-all-start.3
  449.7 18.4 %all-to-all-done.3 = bf16[16,16,2048]{2,0,1:T(8,128)(2,1)S(1)} async-done(((bf16[16,16,2048]{2,0,1:T(8,128)(2,1)}), bf16[16,16,2048]{2,0,1:T(8,128)(2,1)S(1)}, u32[]{:S(2)}, u32[]{:S(2)}) %all-to-all-start.3) | async-done | bytes 1048608 | tf_op jit(solution)/shard_map/all_to_all | solution.py:31
  468.1 1.6 copy.65
  469.7 3.3 reshape.97
  473.0 2.1 pad_maximum_fusion.1
  475.1 10.4 %gather_fusion.3 = bf16[256,64,128]{1,2,0:T(8,128)(2,1)} fusion(bf16[80,64,128]{1,2,0:T(8,128)(2,1)} %pad_maximum_fusion.1, s32[1024]{0:T(1024)S(1)} %pad_clamp_fusion), kind=kCustom, calls=%fused_computation.3 | custom fusion | bytes 8389632 | tf_op jit(solution)/shard_map/gather | solution.py:41
  485.5 9.5 %fusion.58 = f32[256,64,128]{2,1,0:T(8,128)S(1)} fusion(bf16[256,64,128]{1,2,0:T(8,128)(2,1)} %gather_fusion.3, bf16[256,128,128]{2,1,0:T(8,128)(2,1)} %param.12), kind=kOutput, calls=%fused_computation.101 | convolution fusion | flops 536870912 | bytes 20971520 | tf_op jit(solution)/shard_map/kbj,kij->kbi/dot_general | solution.py:42
  495.0 7.5 %fusion = f32[16,64,128]{2,0,1:T(8,128)S(1)} fusion(f32[256,64,128]{2,1,0:T(8,128)S(1)} %fusion.58, s32[256]{0:T(256)S(1)} %copy-done.6, pred[256]{0:T(512)(128)(4,1)S(1)} %iota_compare_fusion.7), kind=kOutput, calls=%fused_computation.4 | convolution fusion | flops 402661376 | bytes 8914176 | tf_op jit(solution)/shard_map/rk,kbi->rbi/dot_general | solution.py:48
  502.5 1.2 convolution_bitcast_fusion.1
  503.7 72.8 %psum.38 = f32[128,64]{0,1:T(8,128)S(1)} all-reduce(f32[128,64]{0,1:T(8,128)S(1)} %convolution_bitcast_fusion.1), channel_id=1, replica_groups=mesh['row'=16,'col'=16] {'row','col'}, use_global_device_ids=true, to_apply=%region_5.8 | all-reduce | flops 8192 | bytes 65536 | tf_op jit(solution)/shard_map/psum | solution.py:66
  576.5 0.7 fusion.13
  577.6 0.7 convolution_bitcast_fusion.3
  578.3 74.5 %psum.39 = f32[64,64]{0,1:T(8,128)S(1)} all-reduce(f32[64,64]{0,1:T(8,128)S(1)} %convolution_bitcast_fusion.3), channel_id=1, replica_groups=mesh['row'=16,'col'=16] {'row','col'}, use_global_device_ids=true, to_apply=%region_6.9 | all-reduce | flops 4096 | bytes 32768 | tf_op jit(solution)/shard_map/psum | solution.py:71
  652.9 5.8 cholesky.81
  660.1 4.9 custom-call.9
  665.3 0.8 convolution_bitcast_fusion
  666.1 1.9 fusion.10
  (56 shorter events, 9.1 us)
Async XLA Ops:
  0.0 1.0 copy-start
  0.0 96.5 %copy-start.5 = (s32[1,256,32]{1,2,0:T(8,128)S(1)}, s32[1,256,32]{1,2,0:T(8,128)}, u32[]{:S(2)}) copy-start(s32[1,256,32]{1,2,0:T(8,128)} %param.16) | copy-start | bytes 98308
  96.8 26.5 %copy-start.7 = (s32[1,256]{1,0:T(1,128)S(1)}, s32[1,256]{1,0:T(1,128)}, u32[]{:S(2)}) copy-start(s32[1,256]{1,0:T(1,128)} %param.17) | copy-start | bytes 3076
  127.3 36.6 %copy-start.3 = (pred[16,16,2048]{2,1,0:T(8,128)(4,1)}, pred[16,16,2048]{2,1,0:T(8,128)(4,1)S(1)}, u32[]{:S(2)}) copy-start(pred[16,16,2048]{2,1,0:T(8,128)(4,1)S(1)} %broadcast_in_dim.17) | copy-start | bytes 1572868
  128.8 39.9 %copy-start.8 = (s32[256]{0:T(256)S(1)}, s32[256]{0:T(256)}, u32[]{:S(2)}) copy-start(s32[256]{0:T(256)} %param.14) | copy-start | bytes 3076
  163.9 21.4 %all-to-all-start.1 = ((bf16[16,16,2048]{2,0,1:T(8,128)(2,1)}), bf16[16,16,2048]{2,0,1:T(8,128)(2,1)S(1)}, u32[]{:S(2)}, u32[]{:S(2)}) async-start(bf16[16,16,2048]{2,0,1:T(8,128)(2,1)} %copy.49), calls=%async_computation.1 | async-start | bytes 2097152 | tf_op jit(solution)/shard_map/all_to_all | solution.py:31
  202.6 9.7 %copy-start.6 = (s32[256]{0:T(256)S(1)}, s32[256]{0:T(256)}, u32[]{:S(2)}) copy-start(s32[256]{0:T(256)} %param.13) | copy-start | bytes 3076
  445.5 22.6 %all-to-all-start.3 = ((bf16[16,16,2048]{2,0,1:T(8,128)(2,1)}), bf16[16,16,2048]{2,0,1:T(8,128)(2,1)S(1)}, u32[]{:S(2)}, u32[]{:S(2)}) async-start(bf16[16,16,2048]{2,0,1:T(8,128)(2,1)} %copy.64), calls=%async_computation.3 | async-start | bytes 2097152 | tf_op jit(solution)/shard_map/all_to_all | solution.py:31
  495.0 7.5 %copy-start.2 = (f32[16,128,64]{1,2,0:T(8,128)S(1)}, f32[16,128,64]{1,2,0:T(8,128)}, u32[]{:S(2)}) copy-start(f32[16,128,64]{1,2,0:T(8,128)} %get-tuple-element.11) | copy-start | bytes 1572868
  502.5 163.6 %copy-start.4 = (f32[192,64]{0,1:T(8,128)S(1)}, f32[192,64]{0,1:T(8,128)}, u32[]{:S(2)}) copy-start(f32[192,64]{0,1:T(8,128)} %param.18) | copy-start | bytes 147460
  502.5 165.5 %copy-start.1 = (f32[16,64,128]{2,1,0:T(8,128)S(1)}, f32[16,64,128]{2,1,0:T(8,128)}, u32[]{:S(2)}) copy-start(f32[16,64,128]{2,1,0:T(8,128)} %param.11) | copy-start | bytes 1572868
where the time goes:
time: 675 us; the launch traced here: 668 us
  blocking collectives  442 us (65%)
  local copies, waits for them, and re-layouts  93.1 us (14%)
  matrix products  45.1 us (7%)
  other arithmetic  44.5 us (7%)
  waiting for transfers between devices  35 us (5%)
  starting transfers between devices  7.75 us (1%)
    psum x2, blocking collectives, body(): lax.psum(local_inner(residual_block, residual_block), ('row', 'col'))  148 us
    psum x2, blocking collectives, body(): lax.psum(local_inner(stacked, product_block), ('row', 'col')) / node_total  146 us
    psum x1, blocking collectives, body(): start_sum = lax.psum(local_inner(start_block, start_block), ('row', 'col'))  81.5 us
    all_to_all x2, blocking collectives, apply_graph(): lax.all_to_all(outgoing, 'row', split_axis=0, concat_axis=0, tiled=True)  66.1 us
    gather x2, local copies, waits for them, and re-layouts, apply_graph(): node_rows[targets.reshape(-1)].reshape(partitions, capacity, block_width)  48.1 us
    all_to_all x2, waiting for transfers between devices, apply_graph(): lax.all_to_all(lax.all_to_all(outgoing, 'row', split_axis=0, concat_axis=...  35 us
    gather x2, local copies, waits for them, and re-layouts, apply_graph(): picked = source[tile_cols]  20.7 us
    another operation x9, other arithmetic, unit_columns(): factor = jnp.linalg.cholesky(gram_matrix)  19.6 us
  transfers between devices with their start and end apart: 2, of which 2 were waited for; matrix products, arithmetic and copies ran while one was open for 0% of the time, Pallas kernels for 0%

commit v1 on v0

--- a/solution.py
+++ b/solution.py
@@ -68,7 +68,10 @@
             "ab,tai->tbi", coefficients, stacked, precision=HIGHEST_PRECISION
         )
         gram_matrix = (
-            lax.psum(local_inner(residual_block, residual_block), ("row", "col")) / node_total
+            jnp.sum(
+                lax.all_gather(local_inner(residual_block, residual_block), ("row", "col")), axis=0
+            )
+            / node_total
         )
         vectors.append(unit_columns(residual_block, gram_matrix))
     all_vectors = jnp.concatenate(vectors, 1)

time: 675 us -> 777 us (1.15)
  waiting for transfers between devices: 35 us -> 261 us
  blocking collectives: 442 us -> 294 us
  between operations: 1.53 us -> 14.7 us
  other arithmetic: 44.5 us -> 52.6 us
    all_gather x0 -> x2, waiting for transfers between devices: none -> 227 us  [body(): lax.all_gather(local_inner(residual_block, residual_block), ('row', 'col'))]
    psum x2 -> x0, blocking collectives: 148 us -> none  [body(): lax.psum(local_inner(residual_block, residual_block), ('row', 'col'))]
    reduce_sum x0 -> x2, other arithmetic: none -> 8.09 us  [body(): jnp.sum(lax.all_gather(local_inner(residual_block, residual_block), ('row...]
  transfers between devices with their start and end apart: 2 -> 4, of which waited for: 2 -> 4; matrix products, arithmetic and copies ran while one was open for 0% -> 0% of each run, Pallas kernels for 0% -> 0%
where the time goes in v1:
time: 777 us; the launch traced here: 771 us
  blocking collectives  294 us (38%)
  waiting for transfers between devices  261 us (34%)
  local copies, waits for them, and re-layouts  93.7 us (12%)
  other arithmetic  52.6 us (7%)
  matrix products  46 us (6%)
  between operations  14.7 us (2%)
  starting transfers between devices  8.71 us (1%)
    all_gather x2, waiting for transfers between devices, body(): lax.all_gather(local_inner(residual_block, residual_block), ('row', 'col'))  227 us
    psum x2, blocking collectives, body(): lax.psum(local_inner(stacked, product_block), ('row', 'col')) / node_total  146 us
    psum x1, blocking collectives, body(): start_sum = lax.psum(local_inner(start_block, start_block), ('row', 'col'))  81.5 us
    all_to_all x2, blocking collectives, apply_graph(): lax.all_to_all(outgoing, 'row', split_axis=0, concat_axis=0, tiled=True)  66.4 us
    gather x2, local copies, waits for them, and re-layouts, apply_graph(): node_rows[targets.reshape(-1)].reshape(partitions, capacity, block_width)  48.1 us
    all_to_all x2, waiting for transfers between devices, apply_graph(): lax.all_to_all(lax.all_to_all(outgoing, 'row', split_axis=0, concat_axis=...  34.7 us
    gather x2, local copies, waits for them, and re-layouts, apply_graph(): picked = source[tile_cols]  20.7 us
    another operation x9, other arithmetic, unit_columns(): factor = jnp.linalg.cholesky(gram_matrix)  19.6 us
  transfers between devices with their start and end apart: 4, of which 4 were waited for; matrix products, arithmetic and copies ran while one was open for 0% of the time, Pallas kernels for 0%

profile of v1, /device:TPU:1, one launch (start us, length us, event | category | flops | bytes accessed | tf_op | source)
XLA Modules:
  0.0 770.9 jit_solution(11039408814972921626)
XLA Ops:
  6.5 1.0 copy-done
  8.1 81.5 %psum.21 = f32[64,64]{0,1:T(8,128)S(1)} all-reduce(f32[64,64]{0,1:T(8,128)S(1)} %convolution_bitcast_fusion.8), channel_id=1, replica_groups=mesh['row'=16,'col'=16] {'row','col'}, use_global_device_ids=true, to_apply=%region_0.0 | all-reduce | flops 4096 | bytes 32768 | tf_op jit(solution)/shard_map/psum | solution.py:59
  89.7 5.8 cholesky.59
  96.9 4.9 custom-call.7
  103.4 24.0 %gather_fusion = bf16[8192,64]{1,0:T(8,128)(2,1)S(1)} fusion(bf16[2048,64]{1,0:T(8,128)(2,1)S(1)} %bitcast.94, s32[8192]{0:T(1024)S(1)} %broadcast_clamp_fusion), kind=kCustom, calls=%fused_computation | custom fusion | bytes 2129920 | tf_op jit(solution)/shard_map/gather | solution.py:27
  127.4 2.4 reshape.93
  130.0 2.1 broadcast_in_dim.16
  132.0 1.8 broadcast_in_dim.17
  133.8 1.5 broadcast_select_fusion.1
  135.4 33.5 %all_to_all.20 = bf16[16,16,2048]{2,1,0:T(8,128)(2,1)S(1)} all-to-all(bf16[16,16,2048]{2,1,0:T(8,128)(2,1)S(1)} %broadcast_select_fusion.1), channel_id=1, replica_groups=mesh['row'=16,'col'=16] {'row'}, dimensions={0} | all-to-all | bytes 2097152 | tf_op jit(solution)/shard_map/all_to_all | solution.py:32
  168.8 1.6 copy.45
  170.4 3.7 all-to-all-start.1
  175.3 16.3 %all-to-all-done.1 = bf16[16,16,2048]{2,0,1:T(8,128)(2,1)S(1)} async-done(((bf16[16,16,2048]{2,0,1:T(8,128)(2,1)}), bf16[16,16,2048]{2,0,1:T(8,128)(2,1)S(1)}, u32[]{:S(2)}, u32[]{:S(2)}) %all-to-all-start.1) | async-done | bytes 1048608 | tf_op jit(solution)/shard_map/all_to_all | solution.py:31
  191.6 1.6 copy.46
  193.2 3.3 reshape.94
  196.5 2.1 pad_maximum_fusion
  198.6 10.4 %gather_fusion.1 = bf16[256,64,128]{1,2,0:T(8,128)(2,1)} fusion(bf16[80,64,128]{1,2,0:T(8,128)(2,1)} %pad_maximum_fusion, s32[1024]{0:T(1024)S(1)} %pad_clamp_fusion), kind=kCustom, calls=%fused_computation.1 | custom fusion | bytes 8389632 | tf_op jit(solution)/shard_map/gather | solution.py:41
  209.0 9.5 %fusion.57 = f32[256,64,128]{2,1,0:T(8,128)S(1)} fusion(bf16[256,64,128]{1,2,0:T(8,128)(2,1)} %gather_fusion.1, bf16[256,128,128]{2,1,0:T(8,128)(2,1)} %param.12), kind=kOutput, calls=%fused_computation.100 | convolution fusion | flops 536870912 | bytes 20971520 | tf_op jit(solution)/shard_map/kbj,kij->kbi/dot_general | solution.py:42
  218.5 7.5 fusion.2
  226.7 73.0 %psum.22 = f32[64,64]{0,1:T(8,128)S(1)} all-reduce(f32[64,64]{0,1:T(8,128)S(1)} %convolution_bitcast_fusion.6), channel_id=1, replica_groups=mesh['row'=16,'col'=16] {'row','col'}, use_global_device_ids=true, to_apply=%region_3.0 | all-reduce | flops 4096 | bytes 32768 | tf_op jit(solution)/shard_map/psum | solution.py:66
  300.6 1.3 convolution_bitcast_fusion.5
  301.9 113.4 %all-gather.5.cloned.1.call-done = f32[16384,64]{1,0:T(8,128)} async-done(((f32[64,64]{1,0:T(8,128)}), f32[16384,64]{1,0:T(8,128)}) %all-gather.5.cloned.1.call-update) | async-done | bytes 4194320 | tf_op jit(solution)/shard_map/all_gather | solution.py:72
  415.4 4.0 reduce_sum.18
  419.6 5.8 cholesky.70
  426.9 4.9 custom-call.8
  432.0 1.6 bitcast_convert_fusion
  433.9 24.0 %gather_fusion.2 = bf16[8192,64]{1,0:T(8,128)(2,1)S(1)} fusion(bf16[2048,64]{1,0:T(8,128)(2,1)S(1)} %bitcast.95, s32[8192]{0:T(1024)S(1)} %broadcast_clamp_fusion), kind=kCustom, calls=%fused_computation.2 | custom fusion | bytes 2129920 | tf_op jit(solution)/shard_map/gather | solution.py:27
  458.0 2.4 reshape.96
  460.4 1.5 broadcast_select_fusion
  461.9 32.9 %all_to_all.21 = bf16[16,16,2048]{2,1,0:T(8,128)(2,1)S(1)} all-to-all(bf16[16,16,2048]{2,1,0:T(8,128)(2,1)S(1)} %broadcast_select_fusion), channel_id=1, replica_groups=mesh['row'=16,'col'=16] {'row'}, dimensions={0} | all-to-all | bytes 2097152 | tf_op jit(solution)/shard_map/all_to_all | solution.py:32
  494.8 1.6 copy.60
  496.4 4.8 all-to-all-start.3
  501.6 18.4 %all-to-all-done.3 = bf16[16,16,2048]{2,0,1:T(8,128)(2,1)S(1)} async-done(((bf16[16,16,2048]{2,0,1:T(8,128)(2,1)}), bf16[16,16,2048]{2,0,1:T(8,128)(2,1)S(1)}, u32[]{:S(2)}, u32[]{:S(2)}) %all-to-all-start.3) | async-done | bytes 1048608 | tf_op jit(solution)/shard_map/all_to_all | solution.py:31
  520.0 1.6 copy.61
  521.5 3.8 reshape.97
  525.3 2.1 pad_maximum_fusion.1
  527.4 10.4 %gather_fusion.3 = bf16[256,64,128]{1,2,0:T(8,128)(2,1)} fusion(bf16[80,64,128]{1,2,0:T(8,128)(2,1)} %pad_maximum_fusion.1, s32[1024]{0:T(1024)S(1)} %pad_clamp_fusion), kind=kCustom, calls=%fused_computation.3 | custom fusion | bytes 8389632 | tf_op jit(solution)/shard_map/gather | solution.py:41
  537.7 9.5 %fusion.58 = f32[256,64,128]{2,1,0:T(8,128)S(1)} fusion(bf16[256,64,128]{1,2,0:T(8,128)(2,1)} %gather_fusion.3, bf16[256,128,128]{2,1,0:T(8,128)(2,1)} %param.12), kind=kOutput, calls=%fused_computation.101 | convolution fusion | flops 536870912 | bytes 20971520 | tf_op jit(solution)/shard_map/kbj,kij->kbi/dot_general | solution.py:42
  547.2 7.5 fusion
  554.7 1.2 convolution_bitcast_fusion.1
  555.9 73.0 %psum.23 = f32[128,64]{0,1:T(8,128)S(1)} all-reduce(f32[128,64]{0,1:T(8,128)S(1)} %convolution_bitcast_fusion.1), channel_id=1, replica_groups=mesh['row'=16,'col'=16] {'row','col'}, use_global_device_ids=true, to_apply=%region_5.8 | all-reduce | flops 8192 | bytes 65536 | tf_op jit(solution)/shard_map/psum | solution.py:66
  630.0 1.3 convolution_bitcast_fusion.3
  631.3 113.2 %all-gather.7.cloned.1.call-done = f32[16384,64]{1,0:T(8,128)} async-done(((f32[64,64]{1,0:T(8,128)}), f32[16384,64]{1,0:T(8,128)}) %all-gather.7.cloned.1.call-update) | async-done | bytes 4194320 | tf_op jit(solution)/shard_map/all_gather | solution.py:72
  744.5 4.1 reduce_sum.19
  748.8 5.8 cholesky.81
  755.9 4.9 custom-call.9
  761.1 0.8 convolution_bitcast_fusion
  761.9 1.9 fusion.10
  (64 shorter events, 11.0 us)
Async XLA Ops:
  6.5 1.0 copy-start
  6.5 96.5 %copy-start.5 = (s32[1,256,32]{1,2,0:T(8,128)S(1)}, s32[1,256,32]{1,2,0:T(8,128)}, u32[]{:S(2)}) copy-start(s32[1,256,32]{1,2,0:T(8,128)} %param.16) | copy-start | bytes 98308
  103.3 26.5 %copy-start.7 = (s32[1,256]{1,0:T(1,128)S(1)}, s32[1,256]{1,0:T(1,128)}, u32[]{:S(2)}) copy-start(s32[1,256]{1,0:T(1,128)} %param.17) | copy-start | bytes 3076
  133.8 36.6 %copy-start.3 = (pred[16,16,2048]{2,1,0:T(8,128)(4,1)}, pred[16,16,2048]{2,1,0:T(8,128)(4,1)S(1)}, u32[]{:S(2)}) copy-start(pred[16,16,2048]{2,1,0:T(8,128)(4,1)S(1)} %broadcast_in_dim.17) | copy-start | bytes 1572868
  135.4 39.9 %copy-start.8 = (s32[256]{0:T(256)S(1)}, s32[256]{0:T(256)}, u32[]{:S(2)}) copy-start(s32[256]{0:T(256)} %param.14) | copy-start | bytes 3076
  170.4 21.2 %all-to-all-start.1 = ((bf16[16,16,2048]{2,0,1:T(8,128)(2,1)}), bf16[16,16,2048]{2,0,1:T(8,128)(2,1)S(1)}, u32[]{:S(2)}, u32[]{:S(2)}) async-start(bf16[16,16,2048]{2,0,1:T(8,128)(2,1)} %copy.45), calls=%async_computation.1 | async-start | bytes 2097152 | tf_op jit(solution)/shard_map/all_to_all | solution.py:31
  174.1 241.3 %all-gather.5.cloned.1.call-start = ((), (), s32[]{:S(2)}) async-start(), calls=%async_computation.4 | async-start | bytes 8421376 | tf_op jit(solution)/shard_map/all_gather | solution.py:72
  209.0 9.5 %copy-start.6 = (s32[256]{0:T(256)S(1)}, s32[256]{0:T(256)}, u32[]{:S(2)}) copy-start(s32[256]{0:T(256)} %param.13) | copy-start | bytes 3076
  496.4 23.5 %all-to-all-start.3 = ((bf16[16,16,2048]{2,0,1:T(8,128)(2,1)}), bf16[16,16,2048]{2,0,1:T(8,128)(2,1)S(1)}, u32[]{:S(2)}, u32[]{:S(2)}) async-start(bf16[16,16,2048]{2,0,1:T(8,128)(2,1)} %copy.60), calls=%async_computation.3 | async-start | bytes 2097152 | tf_op jit(solution)/shard_map/all_to_all | solution.py:31
  501.2 243.3 %all-gather.7.cloned.1.call-start = ((), (), s32[]{:S(2)}) async-start(), calls=%async_computation.5 | async-start | bytes 8421376 | tf_op jit(solution)/shard_map/all_gather | solution.py:72
  547.2 7.5 copy-start.2
  744.5 19.3 %copy-start.1 = (f32[16,64,128]{2,1,0:T(8,128)S(1)}, f32[16,64,128]{2,1,0:T(8,128)}, u32[]{:S(2)}) copy-start(f32[16,64,128]{2,1,0:T(8,128)} %param.11) | copy-start | bytes 1572868
  744.5 17.4 %copy-start.4 = (f32[192,64]{0,1:T(8,128)S(1)}, f32[192,64]{0,1:T(8,128)}, u32[]{:S(2)}) copy-start(f32[192,64]{0,1:T(8,128)} %param.18) | copy-start | bytes 147460
Sparse Core Ops, SparseCore 0:
  302.0 113.2 all-gather.4
  631.5 112.9 all-gather.6
